TPU v7x, 256 devices: a whole 4x4x8 slice. The times are simulated.
256 devices in a mesh: slab: 4 (over x), panel: 64 (over z, y, core).
Axes of the slice: x: 4, y: 4, z: 8, core: 2. Of those that a mesh axis runs over, the one named last changes fastest.
Arguments:
- trial: bfloat16 [1600, 6400], P('slab', 'panel'), may hold values from -6 to 6
- integrals: bfloat16 [6400, 256, 300], P(None, 'panel'), may hold values from -0.078125 to 0.078125
- basis: bfloat16 [2, 1600, 256, 300], P(None, 'slab', 'panel'), may hold values from -0.00048828125 to 0.00048828125
- images: bfloat16 [2, 1600, 256, 300], P(None, 'slab', 'panel'), may hold values from -6 to 6
- current: bfloat16 [1600, 256, 300], P('slab', 'panel'), may hold values from -18 to 18
- occ_energy: float32 [40], replicated, may hold values from -1 to -0.3
- vir_energy: float32 [300], replicated, may hold values from 0.1 to 2
- shift: float32 [1], replicated, may hold values from 0.5 to 1.5
Outputs:
- sigma: bfloat16 [1600, 256, 300], P('slab', 'panel')
- update: bfloat16 [1600, 256, 300], P('slab', 'panel')
- correlations: float32 [2], replicated
All inputs are finite; a program needn't handle non-finite values.
Results may differ from a plain program's by a relative error of at most 0.0079.
Values may be sent and summed in bfloat16 or wider, within the bound.
No kernel may reach another device: no remote copies, remote signals or barrier semaphores. Data moves between devices by JAX's collectives and lax.ppermute only.
A program may use at most 128 MiB of HBM per device.

v0:
```python
import functools

import jax
import jax.numpy as jnp
from jax import lax
from jax.experimental import pallas as pl
from jax.experimental.pallas import tpu as pltpu
from jax.sharding import Mesh, PartitionSpec as P


OCCUPIED = 40
LANES = 128
ROWS = 400
HALF = 200
OWN = 100
SPAN = 800
TILES = 7
WIDE = TILES * LANES
B = 4
A = 300
APAD = 384
DEVICES = 256
GROUPS = (((0, 0),), ((1, 0), (0, 1)), ((2, 0), (0, 2)), ((3, 0), (0, 3)), ((4, 0),))


VMEM = pl.BlockSpec(memory_space=pltpu.VMEM)
SMEM = pl.BlockSpec(memory_space=pltpu.SMEM)
ANY = pl.BlockSpec(memory_space=pl.ANY)


def params(mib):
    return pltpu.CompilerParams(vmem_limit_bytes=mib << 20)


def near(array):
    return pltpu.with_memory_space_constraint(array, pltpu.VMEM)


def lay_kernel(at, *refs):
    pieces, whole = refs[:4], refs[4]
    z, y, c = at[0], at[1], at[2]
    start = lax.rem(z * SPAN, LANES)
    lane = lax.broadcasted_iota(jnp.int32, (OWN, WIDE), 1)
    row = lax.broadcasted_iota(jnp.int32, (OWN, WIDE), 0)
    gap = lane - row - start
    total = jnp.zeros((HALF, WIDE), jnp.float32)
    for dy in range(4):
        for dc in range(2):
            core = c if dc == 0 else 1 - c
            slot = lax.rem(y + 4 - dy, 4) * 2 + core
            pick = jnp.where(gap == slot * OWN, 1.0, 0.0).astype(jnp.bfloat16)
            total += jnp.dot(pieces[dy][dc], pick, preferred_element_type=jnp.float32)
    whole[...] = total.astype(jnp.bfloat16)


def lay(at, pieces):
    return pl.pallas_call(
        lay_kernel,
        out_shape=jax.ShapeDtypeStruct((HALF, WIDE), jnp.bfloat16),
        in_specs=[SMEM] + [VMEM] * 4,
        out_specs=VMEM,
        compiler_params=params(10),
        name="lay",
    )(at, *map(near, pieces))


def gather(pieces, left):
    for i in range(len(pieces) // 2):
        left[i, 0:HALF, :] = pieces[2 * i][...]
        left[i, HALF:ROWS, :] = pieces[2 * i + 1][...]


def part(at, where, native):
    source = lax.rem(at[0] + 8 - where[0] + where[1], 8)
    return native.at[:, :, pl.ds(pl.multiple_of(source * SPAN // LANES * LANES, LANES), WIDE)]


def product(left, right):
    return lax.dot_general(
        left,
        right.reshape(A * B, WIDE),
        (((1,), (1,)), ((), ())),
        preferred_element_type=jnp.float32,
    )


def multiply_kernel(group, first, at, *refs):
    n = len(group)
    pieces, native = refs[: 2 * n], refs[2 * n]
    total, left, right, sems = refs[-4:]
    copies = [
        pltpu.make_async_copy(part(at, group[i], native), right.at[i], sems.at[i]) for i in range(n)
    ]
    for copy in copies:
        copy.start()
    gather(pieces, left)
    for i in range(n):
        copies[i].wait()
        if i == 0 and first:
            total[...] = product(left[i], right[i])
        else:
            old = refs[2 * n + 1] if i == 0 else total
            total[...] = old[...] + product(left[i], right[i])


def multiply(at, group, pieces, native, old):
    n = len(group)
    first = old is None
    return pl.pallas_call(
        functools.partial(multiply_kernel, group, first),
        out_shape=jax.ShapeDtypeStruct((ROWS, A * B), jnp.float32),
        in_specs=[SMEM] + [VMEM] * (2 * n) + [ANY] + ([] if first else [VMEM]),
        out_specs=VMEM,
        scratch_shapes=[
            pltpu.VMEM((n, ROWS, WIDE), jnp.bfloat16),
            pltpu.VMEM((n, A, B, WIDE), jnp.bfloat16),
            pltpu.SemaphoreType.DMA((n,)),
        ],
        input_output_aliases={} if first else {2 * n + 2: 0},
        cost_estimate=pl.CostEstimate(
            flops=2 * n * ROWS * WIDE * B * A, bytes_accessed=n * 3000000, transcendentals=0
        ),
        compiler_params=params(12),
        name="multiply",
    )(at, *map(near, pieces), native, *([] if first else [near(old)]))


CHUNK = 40
CHUNKS = ROWS // CHUNK
SPREAD = APAD // LANES


def fold(x):
    return jnp.sum(x.reshape(CHUNK * B // 8, 8, A), axis=0)


def flat(x):
    return x.reshape(CHUNK * B, A).astype(jnp.float32)


def chunk(i):
    pairs = pl.ds(pl.multiple_of(i * CHUNK, CHUNK), CHUNK)
    rows = pl.ds(pl.multiple_of(i * CHUNK * B, CHUNK * B), CHUNK * B)
    return pairs, rows


def gather_sums(sums, first):
    lane = lax.broadcasted_iota(jnp.int32, (1, LANES), 1)
    line = jnp.zeros((1, LANES), jnp.float32)
    for k, s in enumerate(sums):
        line = jnp.where(lane == first + k, jnp.sum(s, axis=(0, 1), keepdims=True), line)
    return line


def gram_kernel(where, at, virt, row_term, images, native, inverse, line, right, sem):
    copy = pltpu.make_async_copy(part(at, where, native), right, sem)
    copy.start()
    virtual = virt[...]

    def body(i, sums):
        pairs, rows = chunk(i)
        below = 1.0 / jnp.maximum(virtual + row_term[rows, :], 1.0)
        inverse[rows, :] = below
        v0 = flat(images[0, pairs]) * below
        v1 = flat(images[1, pairs]) * below
        return tuple(s + fold(x) for s, x in zip(sums, (v0 * v0, v0 * v1, v1 * v1)))

    zero = jnp.zeros((8, A), jnp.float32)
    line[...] = gather_sums(lax.fori_loop(0, CHUNKS, body, (zero,) * 3), 5)
    copy.wait()


def gram(at, where, virt, row_term, images, native):
    return pl.pallas_call(
        functools.partial(gram_kernel, where),
        out_shape=(
            jax.ShapeDtypeStruct((ROWS * B, A), jnp.float32),
            jax.ShapeDtypeStruct((1, LANES), jnp.float32),
            jax.ShapeDtypeStruct((A, B, WIDE), jnp.bfloat16),
        ),
        in_specs=[SMEM] + [VMEM] * 3 + [ANY],
        out_specs=(VMEM,) * 3,
        scratch_shapes=[pltpu.SemaphoreType.DMA],
        cost_estimate=pl.CostEstimate(flops=20 * ROWS * B * A, bytes_accessed=8000000, transcendentals=0),
        compiler_params=params(2),
        name="gram",
    )(at, *map(near, (virt, row_term, images)), native)


def last_kernel(group, at, *refs):
    n = len(group)
    pieces, right = refs[: 2 * n], refs[2 * n]
    old, shift, inverse, line, basis, images, current = refs[2 * n + 1 : 2 * n + 8]
    sigma, parts = refs[2 * n + 8 : 2 * n + 10]
    left, order, spread, sigma_v, out_sems = refs[2 * n + 10 :]
    wide = B * LANES
    come = lax.broadcasted_iota(jnp.int32, (wide, wide), 0)
    goes = lax.broadcasted_iota(jnp.int32, (wide, wide), 1)
    hit = come == lax.rem(goes, LANES) * B + goes // LANES
    order[...] = jnp.where(hit, 1.0, 0.0).astype(jnp.bfloat16)
    gather(pieces, left)
    rounded = (old[...] + product(left[0], right[...])).astype(jnp.bfloat16)
    rounded = jnp.concatenate(
        [rounded, jnp.zeros((ROWS, (APAD - A) * B), jnp.bfloat16)], axis=1
    )
    for t in range(SPREAD):
        run = rounded[:, t * wide : (t + 1) * wide]
        moved = jnp.dot(run, order[...], preferred_element_type=jnp.float32)
        for b in range(B):
            spread[t, pl.ds(b, ROWS, stride=B), :] = moved[:, b * LANES : (b + 1) * LANES]
    core = at[2]
    shifted = shift[0]

    def out_copy(i):
        pairs, _ = chunk(i)
        return pltpu.make_async_copy(sigma_v.at[pairs], sigma.at[pairs], out_sems.at[i])

    def body(i, sums):
        pairs, rows = chunk(i)
        from_row = lax.rem(i * CHUNK + HALF * core, ROWS) * B
        taken = pl.ds(pl.multiple_of(from_row, CHUNK * B), CHUNK * B)
        sig = jnp.concatenate([spread[t, taken, :] for t in range(SPREAD)], axis=1)[:, :A]
        sigma_v[pairs] = sig.astype(jnp.bfloat16).reshape(CHUNK, B, A)
        out_copy(i).start()
        below = inverse[rows, :]
        u = (sig - shifted * flat(current[pairs])) * below
        w = u * below
        new = (
            flat(basis[0, pairs]) * sig,
            flat(basis[1, pairs]) * sig,
            u * u,
            w * flat(images[0, pairs]),
            w * flat(images[1, pairs]),
        )
        return tuple(s + fold(x) for s, x in zip(sums, new))

    zero = jnp.zeros((8, A), jnp.float32)
    sums = lax.fori_loop(0, CHUNKS, body, (zero,) * 5)
    parts[...] = jnp.broadcast_to((gather_sums(sums, 0) + line[...])[None], (DEVICES, 1, LANES))
    for i in range(CHUNKS):
        out_copy(i).wait()


def last(at, group, pieces, right, old, shift, inverse, line, basis, images, current):
    n = len(group)
    return pl.pallas_call(
        functools.partial(last_kernel, group),
        out_shape=(
            jax.ShapeDtypeStruct((ROWS, B, A), jnp.bfloat16),
            jax.ShapeDtypeStruct((DEVICES, 1, LANES), jnp.float32),
        ),
        in_specs=[SMEM] + [VMEM] * (2 * n + 2) + [SMEM] + [VMEM] * 5,
        out_specs=(ANY, VMEM),
        scratch_shapes=[
            pltpu.VMEM((n, ROWS, WIDE), jnp.bfloat16),
            pltpu.VMEM((B * LANES, B * LANES), jnp.bfloat16),
            pltpu.VMEM((SPREAD, ROWS * B, LANES), jnp.float32),
            pltpu.VMEM((ROWS, B, A), jnp.bfloat16),
            pltpu.SemaphoreType.DMA((CHUNKS,)),
        ],
        compiler_params=params(14),
        name="last",
    )(at, *map(near, pieces), near(right), near(old), shift, *map(near, (inverse, line, basis, images, current)))


def finish_kernel(gathered, shift, inverse, sigma, current, images, update, overlap, flag, update_v, out_sems):
    line = jnp.sum(gathered[...], axis=0)
    lane = lax.broadcasted_iota(jnp.int32, (1, LANES), 1)
    c0, c1, uu, uv0, uv1, v00, v01, v11 = (
        jnp.sum(jnp.where(lane == k, line, 0.0), axis=1, keepdims=True) for k in range(8)
    )
    expanded = uu - 2.0 * (c0 * uv0 + c1 * uv1) + c0 * c0 * v00 + 2.0 * c0 * c1 * v01 + c1 * c1 * v11
    terms = uu + c0 * c0 * v00 + c1 * c1 * v11
    overlap[0] = c0[0, 0]
    overlap[1] = c1[0, 0]
    flag[0] = jnp.where(expanded < 1e-3 * terms, 1.0, 0.0)[0, 0]
    scale = lax.rsqrt(jnp.maximum(expanded, 0.0) + 1e-06)
    shifted = shift[0]

    def out_copy(i):
        pairs, _ = chunk(i)
        return pltpu.make_async_copy(update_v.at[pairs], update.at[pairs], out_sems.at[i])

    def body(i, nothing):
        pairs, rows = chunk(i)
        resid = flat(sigma[pairs]) - shifted * flat(current[pairs])
        resid = resid - c0 * flat(images[0, pairs]) - c1 * flat(images[1, pairs])
        delta = resid * inverse[rows, :]
        update_v[pairs] = (delta * scale).astype(jnp.bfloat16).reshape(CHUNK, B, A)
        out_copy(i).start()
        return nothing

    lax.fori_loop(0, CHUNKS, body, 0)
    for i in range(CHUNKS):
        out_copy(i).wait()


def finish(gathered, shift, inverse, sigma, current, images):
    return pl.pallas_call(
        finish_kernel,
        out_shape=(
            jax.ShapeDtypeStruct((ROWS, B, A), jnp.bfloat16),
            jax.ShapeDtypeStruct((2,), jnp.float32),
            jax.ShapeDtypeStruct((1,), jnp.float32),
        ),
        in_specs=[VMEM, SMEM] + [VMEM] * 4,
        out_specs=(ANY, SMEM, SMEM),
        scratch_shapes=[pltpu.VMEM((ROWS, B, A), jnp.bfloat16), pltpu.SemaphoreType.DMA((CHUNKS,))],
        compiler_params=params(6),
        name="finish",
    )(near(gathered), shift, *map(near, (inverse, sigma, current, images)))


def ring(n, step):
    return [(i, (i + step) % n) for i in range(n)]


SWAP = [(0, 1), (1, 0)]


def per_device(trial, integrals, basis, images, current, occ_energy, vir_energy, shift):
    x, z, y, c = (lax.axis_index(name) for name in "xzyc")
    mine = lax.dynamic_slice_in_dim(trial, HALF * c, HALF, 0)
    other = lax.dynamic_slice_in_dim(trial, HALF * (1 - c), HALF, 0)
    pair = jnp.stack([mine, lax.ppermute(other, "c", SWAP)])
    pieces = [pair] + [lax.ppermute(pair, "y", ring(4, dy)) for dy in (1, 2, 3)]
    at = jnp.stack([z, y, c]).astype(jnp.int32)
    native = pltpu.with_memory_space_constraint(jnp.transpose(integrals, (2, 1, 0)), pltpu.HBM)
    spans = {(0, 0): lay(at, pieces)}
    for k in (1, 2, 3, 4):
        for there, back, step in ((k, 0, 1), (0, k, -1))[: 2 if k < 4 else 1]:
            before = spans[(max(there - 1, 0), max(back - 1, 0))]
            spans[(there, back)] = lax.ppermute(before, "z", ring(8, step))

    def operands(group):
        arrays = []
        for where in group:
            arrays += [spans[where], lax.ppermute(spans[where], "c", SWAP)]
        return arrays

    total = None
    for group in GROUPS[:-1]:
        arrays = operands(group)
        total = multiply(at, group, arrays, native, total)

    global_row = x * ROWS + jnp.arange(ROWS, dtype=jnp.int32)
    orbitals = jnp.arange(OCCUPIED, dtype=jnp.int32)[None, :]
    first = (global_row // OCCUPIED)[:, None] == orbitals
    second = (global_row % OCCUPIED)[:, None] == orbitals
    pair_energy = jnp.sum(jnp.where(first, occ_energy[None, :], 0.0), axis=1) + jnp.sum(
        jnp.where(second, occ_energy[None, :], 0.0), axis=1
    )
    panel = z * 8 + y * 2 + c
    energy_b = lax.dynamic_slice_in_dim(vir_energy, panel * B, B, 0)
    row_term = (energy_b[None, :] - pair_energy[:, None] - shift[0]).reshape(ROWS * B, 1)
    virt = vir_energy[None, :]
    inverse, line, right = gram(at, GROUPS[-1][0], virt, row_term, images, native)
    sigma, parts = last(
        at, GROUPS[-1], operands(GROUPS[-1]), right, total, shift, inverse, line, basis, images, current
    )
    everyone = ("x", "z", "y", "c")
    gathered = lax.all_to_all(parts, everyone, 0, 0, tiled=True)
    update, overlap, flag = finish(gathered, shift, inverse, sigma, current, images)

    def direct(_):
        resid = sigma.astype(jnp.float32) - shift[0] * current.astype(jnp.float32)
        for k in range(2):
            resid = resid - overlap[k] * images[k].astype(jnp.float32)
        delta = resid / jnp.maximum(virt[None] + row_term.reshape(ROWS, B, 1), 1.0)
        size_sq = lax.psum(jnp.sum(delta * delta), everyone)
        return (0.0, (delta * lax.rsqrt(size_sq + 1e-06)).astype(jnp.bfloat16))

    _, update = lax.while_loop(lambda state: state[0] > 0.5, direct, (flag[0], update))
    return (sigma, update, overlap)


def solution(mesh):
    fine = Mesh(mesh.devices.reshape(4, 8, 4, 2), ("x", "z", "y", "c"))
    panel = ("z", "y", "c")
    in_specs = (
        P("x", panel),
        P(None, panel, None),
        P(None, "x", panel, None),
        P(None, "x", panel, None),
        P("x", panel, None),
        P(),
        P(),
        P(),
    )
    out_specs = (P("x", panel, None), P("x", panel, None), P())

    return jax.shard_map(
        per_device, mesh=fine, in_specs=in_specs, out_specs=out_specs, check_vma=False
    )
```

profile of v0, /device:TPU:1, one launch (start us, length us, event | category | flops | bytes accessed | tf_op | source)
XLA Modules:
  0.0 116.9 jit_solution(16762156289853175053)
XLA Ops:
  0.6 1.0 dynamic-slice_bitcast_fusion
  1.6 3.3 %collective-permute-start = (bf16[200,100]{1,0:T(8,128)(2,1)S(1)}, bf16[200,100]{1,0:T(8,128)(2,1)S(1)}, u32[]{:S(2)}, u32[]{:S(2)}) collective-permute-start(bf16[200,100]{1,0:T(8,128)(2,1)S(1)} %get-tuple-element.119), channel_id=1, source_target_pairs={{0,1},{1,0},{2,3},{3,2},{4,5},{5,4},{6,7},{7,6},{8,9},{9,8},{10,11... | collective-permute-start | bytes 120008 | tf_op jit(solution)/shard_map/ppermute | solution.py:325
  4.9 0.9 collective-permute-done
  5.9 2.2 %collective-permute-start.2 = (bf16[2,200,100]{2,1,0:T(8,128)(2,1)S(1)}, bf16[2,200,100]{2,1,0:T(8,128)(2,1)S(1)}, u32[]{:S(2)}, u32[]{:S(2)}) collective-permute-start(bf16[2,200,100]{2,1,0:T(8,128)(2,1)S(1)} %pad_maximum_fusion.refs_0_), channel_id=1, source_target_pairs={{0,4},{2,6},{4,0},{6,2},{1,5},{3,7},{5,1},{7,3},{8,12},{10,14},{12... | collective-permute-start | bytes 240008 | tf_op jit(solution)/shard_map/ppermute | solution.py:326
  8.1 1.1 collective-permute-start.3
  9.3 2.4 %collective-permute-done.1.refs_1_ = bf16[2,200,100]{2,1,0:T(8,128)(2,1)S(1)} collective-permute-done((bf16[2,200,100]{2,1,0:T(8,128)(2,1)S(1)}, bf16[2,200,100]{2,1,0:T(8,128)(2,1)S(1)}, u32[]{:S(2)}, u32[]{:S(2)}) %collective-permute-start.1) | collective-permute-done | bytes 80032 | tf_op jit(solution)/shard_map/ppermute | solution.py:326
  11.7 1.3 %collective-permute-done.2.refs_2_ = bf16[2,200,100]{2,1,0:T(8,128)(2,1)S(1)} collective-permute-done((bf16[2,200,100]{2,1,0:T(8,128)(2,1)S(1)}, bf16[2,200,100]{2,1,0:T(8,128)(2,1)S(1)}, u32[]{:S(2)}, u32[]{:S(2)}) %collective-permute-start.2) | collective-permute-done | bytes 80032 | tf_op jit(solution)/shard_map/ppermute | solution.py:326
  12.9 0.8 collective-permute-done.3.refs_3_
  13.7 1.6 %lay.1.refs_0_ = bf16[200,896]{1,0:T(8,128)(2,1)S(1)} custom-call(s32[3]{0:T(128)S(1)} %pad_add_fusion.at, bf16[2,200,100]{2,1,0:T(8,128)(2,1)S(1)} %pad_maximum_fusion.refs_0_, bf16[2,200,100]{2,1,0:T(8,128)(2,1)S(1)} %collective-permute-done.1.refs_1_, bf16[2,200,100]{2,1,0:T(8,128)(2,1)S(1)} %collective-permute-done.2.refs_2_, ...), custom_call_target="tpu_custom_call" | custom-call | tf_op jit(solution)/shard_map/lay/pallas_call | solution.py:57
  15.3 1.0 collective-permute-start.4
  16.2 4.0 %collective-permute-start.10 = (bf16[200,896]{1,0:T(8,128)(2,1)S(1)}, bf16[200,896]{1,0:T(8,128)(2,1)}, u32[]{:S(2)}, u32[]{:S(2)}) collective-permute-start(bf16[200,896]{1,0:T(8,128)(2,1)S(1)} %lay.1.refs_0_), channel_id=1, source_target_pairs={{0,56},{8,0},{16,8},{24,16},{32,24},{40,32},{48,40},{56,48},{1,57}... | collective-permute-start | bytes 1075208 | tf_op jit(solution)/shard_map/ppermute | solution.py:333
  20.3 7.5 %collective-permute-done.4.refs_0_ = bf16[200,896]{1,0:T(8,128)(2,1)S(1)} collective-permute-done((bf16[200,896]{1,0:T(8,128)(2,1)S(1)}, bf16[200,896]{1,0:T(8,128)(2,1)S(1)}, u32[]{:S(2)}, u32[]{:S(2)}) %collective-permute-start.4) | collective-permute-done | bytes 358432 | tf_op jit(solution)/shard_map/ppermute | solution.py:333
  27.7 2.7 %collective-permute-start.11 = (bf16[200,896]{1,0:T(8,128)(2,1)}, bf16[200,896]{1,0:T(8,128)(2,1)}, u32[]{:S(2)}, u32[]{:S(2)}) collective-permute-start(bf16[200,896]{1,0:T(8,128)(2,1)} %collective-permute-done.10.refs_2_), channel_id=1, source_target_pairs={{0,56},{8,0},{16,8},{24,16},{32,24},{40,32},{48,40},{56,48},{1,57}... | collective-permute-start | bytes 1075208 | tf_op jit(solution)/shard_map/ppermute | solution.py:333
  30.4 6.8 %collective-permute-done.5.refs_0_ = bf16[200,896]{1,0:T(8,128)(2,1)} collective-permute-done((bf16[200,896]{1,0:T(8,128)(2,1)S(1)}, bf16[200,896]{1,0:T(8,128)(2,1)}, u32[]{:S(2)}, u32[]{:S(2)}) %collective-permute-start.5) | collective-permute-done | bytes 358432 | tf_op jit(solution)/shard_map/ppermute | solution.py:333
  37.2 2.6 %collective-permute-start.18 = (bf16[200,896]{1,0:T(8,128)(2,1)S(1)}, bf16[200,896]{1,0:T(8,128)(2,1)}, u32[]{:S(2)}, u32[]{:S(2)}) collective-permute-start(bf16[200,896]{1,0:T(8,128)(2,1)S(1)} %lay.1.refs_0_), channel_id=1, source_target_pairs={{0,1},{1,0},{2,3},{3,2},{4,5},{5,4},{6,7},{7,6},{8,9},{9,8},{10,11... | collective-permute-start | bytes 1075208 | tf_op jit(solution)/shard_map/ppermute | solution.py:338
  39.8 0.7 copy-done.4
  40.6 0.7 copy-done.6
  41.8 3.0 %collective-permute-start.12 = (bf16[200,896]{1,0:T(8,128)(2,1)}, bf16[200,896]{1,0:T(8,128)(2,1)}, u32[]{:S(2)}, u32[]{:S(2)}) collective-permute-start(bf16[200,896]{1,0:T(8,128)(2,1)} %collective-permute-done.11.refs_2_), channel_id=1, source_target_pairs={{0,56},{8,0},{16,8},{24,16},{32,24},{40,32},{48,40},{56,48},{1,57}... | collective-permute-start | bytes 1075208 | tf_op jit(solution)/shard_map/ppermute | solution.py:333
  44.8 1.2 %collective-permute-done.6.refs_0_ = bf16[200,896]{1,0:T(8,128)(2,1)} collective-permute-done((bf16[200,896]{1,0:T(8,128)(2,1)}, bf16[200,896]{1,0:T(8,128)(2,1)}, u32[]{:S(2)}, u32[]{:S(2)}) %collective-permute-start.6) | collective-permute-done | bytes 358432 | tf_op jit(solution)/shard_map/ppermute | solution.py:333
  46.0 1.3 %select_reduce_fusion = (f32[400]{0:T(512)}, f32[400]{0:T(512)}) fusion(s32[400]{0:T(512)S(1)} %get-tuple-element.120, f32[40]{0:T(128)} %param.15, s32[400]{0:T(512)S(1)} %get-tuple-element.121), kind=kLoop, calls=%fused_computation.9 | loop fusion | flops 95200 | bytes 6560 | tf_op jit(solution)/shard_map/reduce_sum | solution.py:350
  48.0 0.8 dynamic_slice.11
  50.1 3.5 %collective-permute-start.14 = (bf16[200,896]{1,0:T(8,128)(2,1)}, bf16[200,896]{1,0:T(8,128)(2,1)}, u32[]{:S(2)}, u32[]{:S(2)}) collective-permute-start(bf16[200,896]{1,0:T(8,128)(2,1)} %collective-permute-done.5.refs_0_), channel_id=1, source_target_pairs={{0,1},{1,0},{2,3},{3,2},{4,5},{5,4},{6,7},{7,6},{8,9},{9,8},{10,11... | collective-permute-start | bytes 1075208 | tf_op jit(solution)/shard_map/ppermute | solution.py:338
  53.6 0.7 copy-done.8
  54.7 3.1 %gram.1 = (f32[1600,300]{1,0:T(8,128)S(1)}, f32[1,128]{1,0:T(1,128)S(1)}, bf16[300,4,896]{2,1,0:T(4,128)(2,1)S(1)}) custom-call(s32[3]{0:T(128)S(1)} %pad_add_fusion.at, f32[1,300]{1,0:T(1,128)S(1)} %broadcast_in_dim.26.virt, f32[1600,1]{1,0:T(8,128)S(1)} %sub.86.row_term, bf16[2,400,4,300]{3,2,1,0:T(4,128)(2,1)S(1)} %copy-done, bf16[300,4,6400]{2,1,0:T(4,128)(2,1)} %bitcast.23), custom_call_target="tpu_custom_call" | custom-call | flops 9600000 | bytes 8000000 | tf_op jit(solution)/shard_map/gram/pallas_call | solution.py:174
  58.6 3.9 %multiply.4.refs_5_ = f32[400,1200]{1,0:T(8,128)S(1)} custom-call(s32[3]{0:T(128)S(1)} %pad_add_fusion.at, bf16[200,896]{1,0:T(8,128)(2,1)S(1)} %copy-done.5, bf16[200,896]{1,0:T(8,128)(2,1)} %collective-permute-done.18.refs_1_, bf16[300,4,6400]{2,1,0:T(4,128)(2,1)} %bitcast.24), custom_call_target="tpu_custom_call" | custom-call | flops 860160000 | bytes 3000000 | tf_op jit(solution)/shard_map/multiply/pallas_call | solution.py:109
  63.0 5.9 %multiply.5.refs_5_ = f32[400,1200]{1,0:T(8,128)S(1)} custom-call(s32[3]{0:T(128)S(1)} %pad_add_fusion.at, bf16[200,896]{1,0:T(8,128)(2,1)S(1)} %copy-done.7, bf16[200,896]{1,0:T(8,128)(2,1)S(1)} %copy-done.9, bf16[200,896]{1,0:T(8,128)(2,1)} %collective-permute-done.10.refs_2_, ...), custom_call_target="tpu_custom_call", output_to_operand_aliasing={{}: (6, {})} | custom-call | flops 1720320000 | bytes 6000000 | tf_op jit(solution)/shard_map/multiply/pallas_call | solution.py:109
  68.9 6.1 %multiply.6.refs_5_ = f32[400,1200]{1,0:T(8,128)S(1)} custom-call(s32[3]{0:T(128)S(1)} %pad_add_fusion.at, bf16[200,896]{1,0:T(8,128)(2,1)} %collective-permute-done.5.refs_0_, bf16[200,896]{1,0:T(8,128)(2,1)} %collective-permute-done.14.refs_1_, bf16[200,896]{1,0:T(8,128)(2,1)} %collective-permute-done.11.refs_2_, ...), custom_call_target="tpu_custom_call", output_to_operand_aliasing={{}: (6, {})} | custom-call | flops 1720320000 | bytes 6000000 | tf_op jit(solution)/shard_map/multiply/pallas_call | solution.py:109
  75.0 6.0 %multiply.7.refs_3_ = f32[400,1200]{1,0:T(8,128)S(1)} custom-call(s32[3]{0:T(128)S(1)} %pad_add_fusion.at, bf16[200,896]{1,0:T(8,128)(2,1)} %collective-permute-done.6.refs_0_, bf16[200,896]{1,0:T(8,128)(2,1)S(1)} %collective-permute-done.9.refs_1_, bf16[200,896]{1,0:T(8,128)(2,1)} %collective-permute-done.12.refs_2_, ...), custom_call_target="tpu_custom_call", output_to_operand_aliasing={{}: (6, {})} | custom-call | flops 1720320000 | bytes 6000000 | tf_op jit(solution)/shard_map/multiply/pallas_call | solution.py:109
  81.1 8.5 %last.1 = (bf16[400,4,300]{2,1,0:T(4,128)(2,1)S(1)}, f32[256,1,128]{2,1,0:T(1,128)S(1)}) custom-call(s32[3]{0:T(128)S(1)} %pad_add_fusion.at, bf16[200,896]{1,0:T(8,128)(2,1)} %collective-permute-done.7.refs_0_, bf16[200,896]{1,0:T(8,128)(2,1)S(1)} %collective-permute-done.8.refs_1_, bf16[300,4,896]{2,1,0:T(4,128)(2,1)S(1)} %get-tuple-element.56.refs_2_, ...), custom_call_target="tpu_custom_call" | custom-call | tf_op jit(solution)/shard_map/last/pallas_call | solution.py:246
  89.6 22.7 %all_to_all.5.gathered = f32[256,1,128]{2,1,0:T(1,128)S(1)} all-to-all(f32[256,1,128]{2,1,0:T(1,128)S(1)} %get-tuple-element.60), channel_id=1, replica_groups=mesh['x'=4,'z'=8,'y'=4,'c'=2] {'x','z','y','c'}, dimensions={0} | all-to-all | bytes 262144 | tf_op jit(solution)/shard_map/all_to_all | solution.py:362
  112.3 3.4 %finish.1 = (bf16[400,4,300]{2,1,0:T(4,128)(2,1)}, f32[2]{0:T(128)S(1)}, f32[1]{0:T(128)}) custom-call(f32[256,1,128]{2,1,0:T(1,128)S(1)} %all_to_all.5.gathered, f32[1]{0:T(128)} %copy.28.refs_4_.shift, f32[1600,300]{1,0:T(8,128)S(1)} %get-tuple-element.57.refs_5_.inverse, bf16[400,4,300]{2,1,0:T(4,128)(2,1)S(1)} %get-tuple-element.135.sigma, ...), custom_call_target="tpu_custom_call" | custom-call | tf_op jit(solution)/shard_map/finish/pallas_call | solution.py:299
  115.7 0.7 while.10
  (50 shorter events, 4.2 us)
Async XLA Ops:
  0.6 54.1 %copy-start = (bf16[2,400,4,300]{3,2,1,0:T(4,128)(2,1)S(1)}, bf16[2,400,4,300]{3,2,1,0:T(4,128)(2,1)}, u32[]{:S(2)}) copy-start(bf16[2,400,4,300]{3,2,1,0:T(4,128)(2,1)} %images.3) | copy-start | bytes 5760004
  1.6 4.2 %collective-permute-start = (bf16[200,100]{1,0:T(8,128)(2,1)S(1)}, bf16[200,100]{1,0:T(8,128)(2,1)S(1)}, u32[]{:S(2)}, u32[]{:S(2)}) collective-permute-start(bf16[200,100]{1,0:T(8,128)(2,1)S(1)} %get-tuple-element.119), channel_id=1, source_target_pairs={{0,1},{1,0},{2,3},{3,2},{4,5},{5,4},{6,7},{7,6},{8,9},{9,8},{10,11... | collective-permute-start | bytes 120008 | tf_op jit(solution)/shard_map/ppermute | solution.py:325
  5.8 5.8 %collective-permute-start.1 = (bf16[2,200,100]{2,1,0:T(8,128)(2,1)S(1)}, bf16[2,200,100]{2,1,0:T(8,128)(2,1)S(1)}, u32[]{:S(2)}, u32[]{:S(2)}) collective-permute-start(bf16[2,200,100]{2,1,0:T(8,128)(2,1)S(1)} %pad_maximum_fusion.refs_0_), channel_id=1, source_target_pairs={{0,2},{2,4},{4,6},{6,0},{1,3},{3,5},{5,7},{7,1},{8,10},{10,12},{12... | collective-permute-start | bytes 240008 | tf_op jit(solution)/shard_map/ppermute | solution.py:326
  5.9 7.0 %collective-permute-start.2 = (bf16[2,200,100]{2,1,0:T(8,128)(2,1)S(1)}, bf16[2,200,100]{2,1,0:T(8,128)(2,1)S(1)}, u32[]{:S(2)}, u32[]{:S(2)}) collective-permute-start(bf16[2,200,100]{2,1,0:T(8,128)(2,1)S(1)} %pad_maximum_fusion.refs_0_), channel_id=1, source_target_pairs={{0,4},{2,6},{4,0},{6,2},{1,5},{3,7},{5,1},{7,3},{8,12},{10,14},{12... | collective-permute-start | bytes 240008 | tf_op jit(solution)/shard_map/ppermute | solution.py:326
  8.1 5.6 %collective-permute-start.3 = (bf16[2,200,100]{2,1,0:T(8,128)(2,1)S(1)}, bf16[2,200,100]{2,1,0:T(8,128)(2,1)S(1)}, u32[]{:S(2)}, u32[]{:S(2)}) collective-permute-start(bf16[2,200,100]{2,1,0:T(8,128)(2,1)S(1)} %pad_maximum_fusion.refs_0_), channel_id=1, source_target_pairs={{0,6},{2,0},{4,2},{6,4},{1,7},{3,1},{5,3},{7,5},{8,14},{10,8},{12,... | collective-permute-start | bytes 240008 | tf_op jit(solution)/shard_map/ppermute | solution.py:326
  15.3 12.4 %collective-permute-start.4 = (bf16[200,896]{1,0:T(8,128)(2,1)S(1)}, bf16[200,896]{1,0:T(8,128)(2,1)S(1)}, u32[]{:S(2)}, u32[]{:S(2)}) collective-permute-start(bf16[200,896]{1,0:T(8,128)(2,1)S(1)} %lay.1.refs_0_), channel_id=1, source_target_pairs={{0,8},{8,16},{16,24},{24,32},{32,40},{40,48},{48,56},{56,0},{1,9},... | collective-permute-start | bytes 1075208 | tf_op jit(solution)/shard_map/ppermute | solution.py:333
  16.2 11.5 %collective-permute-start.10 = (bf16[200,896]{1,0:T(8,128)(2,1)S(1)}, bf16[200,896]{1,0:T(8,128)(2,1)}, u32[]{:S(2)}, u32[]{:S(2)}) collective-permute-start(bf16[200,896]{1,0:T(8,128)(2,1)S(1)} %lay.1.refs_0_), channel_id=1, source_target_pairs={{0,56},{8,0},{16,8},{24,16},{32,24},{40,32},{48,40},{56,48},{1,57}... | collective-permute-start | bytes 1075208 | tf_op jit(solution)/shard_map/ppermute | solution.py:333
  27.7 9.5 %collective-permute-start.5 = (bf16[200,896]{1,0:T(8,128)(2,1)S(1)}, bf16[200,896]{1,0:T(8,128)(2,1)}, u32[]{:S(2)}, u32[]{:S(2)}) collective-permute-start(bf16[200,896]{1,0:T(8,128)(2,1)S(1)} %collective-permute-done.4.refs_0_), channel_id=1, source_target_pairs={{0,8},{8,16},{16,24},{24,32},{32,40},{40,48},{48,56},{56,0},{1,9},... | collective-permute-start | bytes 1075208 | tf_op jit(solution)/shard_map/ppermute | solution.py:333
  27.7 14.1 %collective-permute-start.11 = (bf16[200,896]{1,0:T(8,128)(2,1)}, bf16[200,896]{1,0:T(8,128)(2,1)}, u32[]{:S(2)}, u32[]{:S(2)}) collective-permute-start(bf16[200,896]{1,0:T(8,128)(2,1)} %collective-permute-done.10.refs_2_), channel_id=1, source_target_pairs={{0,56},{8,0},{16,8},{24,16},{32,24},{40,32},{48,40},{56,48},{1,57}... | collective-permute-start | bytes 1075208 | tf_op jit(solution)/shard_map/ppermute | solution.py:333
  37.2 8.8 %collective-permute-start.6 = (bf16[200,896]{1,0:T(8,128)(2,1)}, bf16[200,896]{1,0:T(8,128)(2,1)}, u32[]{:S(2)}, u32[]{:S(2)}) collective-permute-start(bf16[200,896]{1,0:T(8,128)(2,1)} %collective-permute-done.5.refs_0_), channel_id=1, source_target_pairs={{0,8},{8,16},{16,24},{24,32},{32,40},{40,48},{48,56},{56,0},{1,9},... | collective-permute-start | bytes 1075208 | tf_op jit(solution)/shard_map/ppermute | solution.py:333
  37.2 12.9 %collective-permute-start.18 = (bf16[200,896]{1,0:T(8,128)(2,1)S(1)}, bf16[200,896]{1,0:T(8,128)(2,1)}, u32[]{:S(2)}, u32[]{:S(2)}) collective-permute-start(bf16[200,896]{1,0:T(8,128)(2,1)S(1)} %lay.1.refs_0_), channel_id=1, source_target_pairs={{0,1},{1,0},{2,3},{3,2},{4,5},{5,4},{6,7},{7,6},{8,9},{9,8},{10,11... | collective-permute-start | bytes 1075208 | tf_op jit(solution)/shard_map/ppermute | solution.py:338
  39.8 0.7 copy-start.4
  40.6 13.0 %collective-permute-start.16 = (bf16[200,896]{1,0:T(8,128)(2,1)S(1)}, bf16[200,896]{1,0:T(8,128)(2,1)S(1)}, u32[]{:S(2)}, u32[]{:S(2)}) collective-permute-start(bf16[200,896]{1,0:T(8,128)(2,1)S(1)} %collective-permute-done.4.refs_0_), channel_id=1, source_target_pairs={{0,1},{1,0},{2,3},{3,2},{4,5},{5,4},{6,7},{7,6},{8,9},{9,8},{10,11... | collective-permute-start | bytes 1075208 | tf_op jit(solution)/shard_map/ppermute | solution.py:338
  40.6 0.7 copy-start.6
  41.3 16.6 %collective-permute-start.17 = (bf16[200,896]{1,0:T(8,128)(2,1)}, bf16[200,896]{1,0:T(8,128)(2,1)}, u32[]{:S(2)}, u32[]{:S(2)}) collective-permute-start(bf16[200,896]{1,0:T(8,128)(2,1)} %collective-permute-done.10.refs_2_), channel_id=1, source_target_pairs={{0,1},{1,0},{2,3},{3,2},{4,5},{5,4},{6,7},{7,6},{8,9},{9,8},{10,11... | collective-permute-start | bytes 1075208 | tf_op jit(solution)/shard_map/ppermute | solution.py:338
  41.8 16.6 %collective-permute-start.12 = (bf16[200,896]{1,0:T(8,128)(2,1)}, bf16[200,896]{1,0:T(8,128)(2,1)}, u32[]{:S(2)}, u32[]{:S(2)}) collective-permute-start(bf16[200,896]{1,0:T(8,128)(2,1)} %collective-permute-done.11.refs_2_), channel_id=1, source_target_pairs={{0,56},{8,0},{16,8},{24,16},{32,24},{40,32},{48,40},{56,48},{1,57}... | collective-permute-start | bytes 1075208 | tf_op jit(solution)/shard_map/ppermute | solution.py:333
  46.0 16.5 %collective-permute-start.7 = (bf16[200,896]{1,0:T(8,128)(2,1)}, bf16[200,896]{1,0:T(8,128)(2,1)}, u32[]{:S(2)}, u32[]{:S(2)}) collective-permute-start(bf16[200,896]{1,0:T(8,128)(2,1)} %collective-permute-done.6.refs_0_), channel_id=1, source_target_pairs={{0,8},{8,16},{16,24},{24,32},{32,40},{40,48},{48,56},{56,0},{1,9},... | collective-permute-start | bytes 1075208 | tf_op jit(solution)/shard_map/ppermute | solution.py:333
  50.1 18.7 %collective-permute-start.14 = (bf16[200,896]{1,0:T(8,128)(2,1)}, bf16[200,896]{1,0:T(8,128)(2,1)}, u32[]{:S(2)}, u32[]{:S(2)}) collective-permute-start(bf16[200,896]{1,0:T(8,128)(2,1)} %collective-permute-done.5.refs_0_), channel_id=1, source_target_pairs={{0,1},{1,0},{2,3},{3,2},{4,5},{5,4},{6,7},{7,6},{8,9},{9,8},{10,11... | collective-permute-start | bytes 1075208 | tf_op jit(solution)/shard_map/ppermute | solution.py:338
  53.6 0.7 copy-start.8
  54.4 14.5 %collective-permute-start.15 = (bf16[200,896]{1,0:T(8,128)(2,1)}, bf16[200,896]{1,0:T(8,128)(2,1)}, u32[]{:S(2)}, u32[]{:S(2)}) collective-permute-start(bf16[200,896]{1,0:T(8,128)(2,1)} %collective-permute-done.11.refs_2_), channel_id=1, source_target_pairs={{0,1},{1,0},{2,3},{3,2},{4,5},{5,4},{6,7},{7,6},{8,9},{9,8},{10,11... | collective-permute-start | bytes 1075208 | tf_op jit(solution)/shard_map/ppermute | solution.py:338
  54.7 3.9 %copy-start.5 = (bf16[200,896]{1,0:T(8,128)(2,1)S(1)}, bf16[200,896]{1,0:T(8,128)(2,1)}, u32[]{:S(2)}) copy-start(bf16[200,896]{1,0:T(8,128)(2,1)} %copy-done.4) | copy-start | bytes 1075204
  57.8 5.1 %copy-start.7 = (bf16[200,896]{1,0:T(8,128)(2,1)S(1)}, bf16[200,896]{1,0:T(8,128)(2,1)}, u32[]{:S(2)}) copy-start(bf16[200,896]{1,0:T(8,128)(2,1)} %copy-done.6) | copy-start | bytes 1075204
  57.9 5.1 %copy-start.9 = (bf16[200,896]{1,0:T(8,128)(2,1)S(1)}, bf16[200,896]{1,0:T(8,128)(2,1)}, u32[]{:S(2)}) copy-start(bf16[200,896]{1,0:T(8,128)(2,1)} %copy-done.8) | copy-start | bytes 1075204
  57.9 17.1 %collective-permute-start.9 = (bf16[200,896]{1,0:T(8,128)(2,1)}, bf16[200,896]{1,0:T(8,128)(2,1)S(1)}, u32[]{:S(2)}, u32[]{:S(2)}) collective-permute-start(bf16[200,896]{1,0:T(8,128)(2,1)} %collective-permute-done.6.refs_0_), channel_id=1, source_target_pairs={{0,1},{1,0},{2,3},{3,2},{4,5},{5,4},{6,7},{7,6},{8,9},{9,8},{10,11... | collective-permute-start | bytes 1075208 | tf_op jit(solution)/shard_map/ppermute | solution.py:338
  58.5 16.5 %collective-permute-start.13 = (bf16[200,896]{1,0:T(8,128)(2,1)}, bf16[200,896]{1,0:T(8,128)(2,1)S(1)}, u32[]{:S(2)}, u32[]{:S(2)}) collective-permute-start(bf16[200,896]{1,0:T(8,128)(2,1)} %collective-permute-done.12.refs_2_), channel_id=1, source_target_pairs={{0,1},{1,0},{2,3},{3,2},{4,5},{5,4},{6,7},{7,6},{8,9},{9,8},{10,11... | collective-permute-start | bytes 1075208 | tf_op jit(solution)/shard_map/ppermute | solution.py:338
  62.5 18.5 %collective-permute-start.8 = (bf16[200,896]{1,0:T(8,128)(2,1)}, bf16[200,896]{1,0:T(8,128)(2,1)S(1)}, u32[]{:S(2)}, u32[]{:S(2)}) collective-permute-start(bf16[200,896]{1,0:T(8,128)(2,1)} %collective-permute-done.7.refs_0_), channel_id=1, source_target_pairs={{0,1},{1,0},{2,3},{3,2},{4,5},{5,4},{6,7},{7,6},{8,9},{9,8},{10,11... | collective-permute-start | bytes 1075208 | tf_op jit(solution)/shard_map/ppermute | solution.py:338
  75.0 6.1 %copy-start.1 = (bf16[400,4,300]{2,1,0:T(4,128)(2,1)S(1)}, bf16[400,4,300]{2,1,0:T(4,128)(2,1)}, u32[]{:S(2)}) copy-start(bf16[400,4,300]{2,1,0:T(4,128)(2,1)} %current.1) | copy-start | bytes 2880004
  75.0 6.1 %copy-start.3 = (bf16[2,400,4,300]{3,2,1,0:T(4,128)(2,1)S(1)}, bf16[2,400,4,300]{3,2,1,0:T(4,128)(2,1)}, u32[]{:S(2)}) copy-start(bf16[2,400,4,300]{3,2,1,0:T(4,128)(2,1)} %refs_7_.1) | copy-start | bytes 5760004
  89.6 26.1 %copy-start.2 = (bf16[400,4,300]{2,1,0:T(4,128)(2,1)}, bf16[400,4,300]{2,1,0:T(4,128)(2,1)S(1)}, u32[]{:S(2)}) copy-start(bf16[400,4,300]{2,1,0:T(4,128)(2,1)S(1)} %get-tuple-element.135.sigma) | copy-start | bytes 2880004
  112.3 3.4 %copy-start.10 = (f32[300]{0:T(512)S(1)}, f32[300]{0:T(512)}, u32[]{:S(2)}) copy-start(f32[300]{0:T(512)} %param.16) | copy-start | bytes 3604
  116.4 0.5 copy-start.11
where the time goes:
time: 117 us
  Pallas kernels  38.4 us (33%)
  starting transfers between devices  25.1 us (21%)
  blocking collectives  22.7 us (19%)
  waiting for transfers between devices  20.8 us (18%)
  local copies, waits for them, and re-layouts  5.41 us (5%)
  other arithmetic  2.25 us (2%)
  between operations  1.56 us (1%)
    all_to_all x1, blocking collectives, per_device(): gathered = lax.all_to_all(parts, everyone, 0, 0, tiled=True)  22.7 us
    pallas_call x4, Pallas kernels, multiply(): pl.pallas_call(functools.partial(multiply_kernel, group, first), out_shap...  21.8 us
    ppermute x7, waiting for transfers between devices, per_device(): spans[there, back] = lax.ppermute(before, 'z', ring(8, step))  15.5 us
    ppermute x7, starting transfers between devices, per_device(): spans[there, back] = lax.ppermute(before, 'z', ring(8, step))  10.6 us
    pallas_call x1, Pallas kernels, last(): pl.pallas_call(functools.partial(last_kernel, group), out_shape=(jax.Shap...  8.55 us
    ppermute x8, starting transfers between devices, operands(): arrays += [spans[where], lax.ppermute(spans[where], 'c', SWAP)]  7.83 us
    ppermute x3, waiting for transfers between devices, per_device(): pieces = [pair] + [lax.ppermute(pair, 'y', ring(4, dy)) for dy in (1, 2, 3)]  4.44 us
    pallas_call x1, Pallas kernels, finish(): pl.pallas_call(finish_kernel, out_shape=(jax.ShapeDtypeStruct((ROWS, B, A...  3.38 us
  transfers between devices with their start and end apart: 19, of which 7 were waited for; matrix products, arithmetic and copies ran while one was open for 3% of the time, Pallas kernels for 21%

commit v1 on v0

--- a/solution.py
+++ b/solution.py
@@ -84,45 +84,55 @@
     )
 
 
-def multiply_kernel(group, first, at, *refs):
-    n = len(group)
-    pieces, native = refs[: 2 * n], refs[2 * n]
-    total, left, right, sems = refs[-4:]
+def fetch(at, group, native, right, sems):
     copies = [
-        pltpu.make_async_copy(part(at, group[i], native), right.at[i], sems.at[i]) for i in range(n)
+        pltpu.make_async_copy(part(at, where, native), right.at[i], sems.at[i])
+        for i, where in enumerate(group)
     ]
     for copy in copies:
         copy.start()
+    return copies
+
+
+def parts_of(group):
+    return jax.ShapeDtypeStruct((len(group), A, B, WIDE), jnp.bfloat16)
+
+
+def multiply_kernel(group, following, first, at, *refs):
+    n = len(group)
+    pieces, native, right = refs[: 2 * n], refs[2 * n], refs[2 * n + 1]
+    total, ahead, left, sems = refs[-4:]
+    copies = fetch(at, following, native, ahead, sems)
     gather(pieces, left)
     for i in range(n):
-        copies[i].wait()
         if i == 0 and first:
             total[...] = product(left[i], right[i])
         else:
-            old = refs[2 * n + 1] if i == 0 else total
+            old = refs[2 * n + 2] if i == 0 else total
             total[...] = old[...] + product(left[i], right[i])
-
-
-def multiply(at, group, pieces, native, old):
+    for copy in copies:
+        copy.wait()
+
+
+def multiply(at, group, following, pieces, native, right, old):
     n = len(group)
     first = old is None
     return pl.pallas_call(
-        functools.partial(multiply_kernel, group, first),
-        out_shape=jax.ShapeDtypeStruct((ROWS, A * B), jnp.float32),
-        in_specs=[SMEM] + [VMEM] * (2 * n) + [ANY] + ([] if first else [VMEM]),
-        out_specs=VMEM,
+        functools.partial(multiply_kernel, group, following, first),
+        out_shape=(jax.ShapeDtypeStruct((ROWS, A * B), jnp.float32), parts_of(following)),
+        in_specs=[SMEM] + [VMEM] * (2 * n) + [ANY, VMEM] + ([] if first else [VMEM]),
+        out_specs=(VMEM, VMEM),
         scratch_shapes=[
             pltpu.VMEM((n, ROWS, WIDE), jnp.bfloat16),
-            pltpu.VMEM((n, A, B, WIDE), jnp.bfloat16),
-            pltpu.SemaphoreType.DMA((n,)),
+            pltpu.SemaphoreType.DMA((len(following),)),
         ],
-        input_output_aliases={} if first else {2 * n + 2: 0},
+        input_output_aliases={} if first else {2 * n + 3: 0},
         cost_estimate=pl.CostEstimate(
             flops=2 * n * ROWS * WIDE * B * A, bytes_accessed=n * 3000000, transcendentals=0
         ),
-        compiler_params=params(12),
+        compiler_params=params(8),
         name="multiply",
-    )(at, *map(near, pieces), native, *([] if first else [near(old)]))
+    )(at, *map(near, pieces), native, near(right), *([] if first else [near(old)]))
 
 
 CHUNK = 40
@@ -152,9 +162,8 @@
     return line
 
 
-def gram_kernel(where, at, virt, row_term, images, native, inverse, line, right, sem):
-    copy = pltpu.make_async_copy(part(at, where, native), right, sem)
-    copy.start()
+def gram_kernel(group, at, virt, row_term, images, native, inverse, line, ahead, sems):
+    copies = fetch(at, group, native, ahead, sems)
     virtual = virt[...]
 
     def body(i, sums):
@@ -167,20 +176,21 @@
 
     zero = jnp.zeros((8, A), jnp.float32)
     line[...] = gather_sums(lax.fori_loop(0, CHUNKS, body, (zero,) * 3), 5)
-    copy.wait()
-
-
-def gram(at, where, virt, row_term, images, native):
+    for copy in copies:
+        copy.wait()
+
+
+def gram(at, group, virt, row_term, images, native):
     return pl.pallas_call(
-        functools.partial(gram_kernel, where),
+        functools.partial(gram_kernel, group),
         out_shape=(
             jax.ShapeDtypeStruct((ROWS * B, A), jnp.float32),
             jax.ShapeDtypeStruct((1, LANES), jnp.float32),
-            jax.ShapeDtypeStruct((A, B, WIDE), jnp.bfloat16),
+            parts_of(group),
         ),
         in_specs=[SMEM] + [VMEM] * 3 + [ANY],
         out_specs=(VMEM,) * 3,
-        scratch_shapes=[pltpu.SemaphoreType.DMA],
+        scratch_shapes=[pltpu.SemaphoreType.DMA((len(group),))],
         cost_estimate=pl.CostEstimate(flops=20 * ROWS * B * A, bytes_accessed=8000000, transcendentals=0),
         compiler_params=params(2),
         name="gram",
@@ -199,7 +209,7 @@
     hit = come == lax.rem(goes, LANES) * B + goes // LANES
     order[...] = jnp.where(hit, 1.0, 0.0).astype(jnp.bfloat16)
     gather(pieces, left)
-    rounded = (old[...] + product(left[0], right[...])).astype(jnp.bfloat16)
+    rounded = (old[...] + product(left[0], right[0])).astype(jnp.bfloat16)
     rounded = jnp.concatenate(
         [rounded, jnp.zeros((ROWS, (APAD - A) * B), jnp.bfloat16)], axis=1
     )
@@ -338,11 +348,6 @@
             arrays += [spans[where], lax.ppermute(spans[where], "c", SWAP)]
         return arrays
 
-    total = None
-    for group in GROUPS[:-1]:
-        arrays = operands(group)
-        total = multiply(at, group, arrays, native, total)
-
     global_row = x * ROWS + jnp.arange(ROWS, dtype=jnp.int32)
     orbitals = jnp.arange(OCCUPIED, dtype=jnp.int32)[None, :]
     first = (global_row // OCCUPIED)[:, None] == orbitals
@@ -354,7 +359,11 @@
     energy_b = lax.dynamic_slice_in_dim(vir_energy, panel * B, B, 0)
     row_term = (energy_b[None, :] - pair_energy[:, None] - shift[0]).reshape(ROWS * B, 1)
     virt = vir_energy[None, :]
-    inverse, line, right = gram(at, GROUPS[-1][0], virt, row_term, images, native)
+    inverse, line, right = gram(at, GROUPS[0], virt, row_term, images, native)
+    total = None
+    for k, group in enumerate(GROUPS[:-1]):
+        arrays = operands(group)
+        total, right = multiply(at, group, GROUPS[k + 1], arrays, native, right, total)
     sigma, parts = last(
         at, GROUPS[-1], operands(GROUPS[-1]), right, total, shift, inverse, line, basis, images, current
     )

time: 117 us -> 112 us (0.957)
  Pallas kernels: 38.4 us -> 33.2 us
    pallas_call x5, Pallas kernels: 24.9 us -> 19.6 us  [the longest x4 16.5 us: multiply(): pl.pallas_call(functools.partial(multiply_kernel, group, following, first...]
  transfers between devices with their start and end apart: 19 -> 19, of which waited for: 7 -> 7; matrix products, arithmetic and copies ran while one was open for 3% -> 3% of each run, Pallas kernels for 21% -> 18%
where the time goes in v1:
time: 112 us
  Pallas kernels  33.2 us (30%)
  starting transfers between devices  25.1 us (22%)
  blocking collectives  22.7 us (20%)
  waiting for transfers between devices  20.8 us (19%)
  local copies, waits for them, and re-layouts  5.4 us (5%)
  other arithmetic  2.27 us (2%)
  between operations  1.54 us (1%)
    all_to_all x1, blocking collectives, per_device(): gathered = lax.all_to_all(parts, everyone, 0, 0, tiled=True)  22.7 us
    pallas_call x4, Pallas kernels, multiply(): pl.pallas_call(functools.partial(multiply_kernel, group, following, first...  16.5 us
    ppermute x7, waiting for transfers between devices, per_device(): spans[there, back] = lax.ppermute(before, 'z', ring(8, step))  15.5 us
    ppermute x7, starting transfers between devices, per_device(): spans[there, back] = lax.ppermute(before, 'z', ring(8, step))  10.6 us
    pallas_call x1, Pallas kernels, last(): pl.pallas_call(functools.partial(last_kernel, group), out_shape=(jax.Shap...  8.64 us
    ppermute x8, starting transfers between devices, operands(): arrays += [spans[where], lax.ppermute(spans[where], 'c', SWAP)]  7.83 us
    ppermute x3, waiting for transfers between devices, per_device(): pieces = [pair] + [lax.ppermute(pair, 'y', ring(4, dy)) for dy in (1, 2, 3)]  4.44 us
    pallas_call x1, Pallas kernels, finish(): pl.pallas_call(finish_kernel, out_shape=(jax.ShapeDtypeStruct((ROWS, B, A...  3.39 us
  transfers between devices with their start and end apart: 19, of which 7 were waited for; matrix products, arithmetic and copies ran while one was open for 3% of the time, Pallas kernels for 18%

profile of v1, /device:TPU:1, one launch (start us, length us, event | category | flops | bytes accessed | tf_op | source)
XLA Modules:
  0.0 111.5 jit_solution(17288400951250285147)
XLA Ops:
  0.6 1.0 dynamic-slice_bitcast_fusion
  1.6 3.3 %collective-permute-start = (bf16[200,100]{1,0:T(8,128)(2,1)S(1)}, bf16[200,100]{1,0:T(8,128)(2,1)S(1)}, u32[]{:S(2)}, u32[]{:S(2)}) collective-permute-start(bf16[200,100]{1,0:T(8,128)(2,1)S(1)} %get-tuple-element.135), channel_id=1, source_target_pairs={{0,1},{1,0},{2,3},{3,2},{4,5},{5,4},{6,7},{7,6},{8,9},{9,8},{10,11... | collective-permute-start | bytes 120008 | tf_op jit(solution)/shard_map/ppermute | solution.py:335
  4.9 0.9 collective-permute-done
  5.9 2.2 %collective-permute-start.2 = (bf16[2,200,100]{2,1,0:T(8,128)(2,1)S(1)}, bf16[2,200,100]{2,1,0:T(8,128)(2,1)S(1)}, u32[]{:S(2)}, u32[]{:S(2)}) collective-permute-start(bf16[2,200,100]{2,1,0:T(8,128)(2,1)S(1)} %pad_maximum_fusion.refs_0_), channel_id=1, source_target_pairs={{0,4},{2,6},{4,0},{6,2},{1,5},{3,7},{5,1},{7,3},{8,12},{10,14},{12... | collective-permute-start | bytes 240008 | tf_op jit(solution)/shard_map/ppermute | solution.py:336
  8.1 1.1 collective-permute-start.3
  9.3 2.4 %collective-permute-done.1.refs_1_ = bf16[2,200,100]{2,1,0:T(8,128)(2,1)S(1)} collective-permute-done((bf16[2,200,100]{2,1,0:T(8,128)(2,1)S(1)}, bf16[2,200,100]{2,1,0:T(8,128)(2,1)S(1)}, u32[]{:S(2)}, u32[]{:S(2)}) %collective-permute-start.1) | collective-permute-done | bytes 80032 | tf_op jit(solution)/shard_map/ppermute | solution.py:336
  11.7 1.3 %collective-permute-done.2.refs_2_ = bf16[2,200,100]{2,1,0:T(8,128)(2,1)S(1)} collective-permute-done((bf16[2,200,100]{2,1,0:T(8,128)(2,1)S(1)}, bf16[2,200,100]{2,1,0:T(8,128)(2,1)S(1)}, u32[]{:S(2)}, u32[]{:S(2)}) %collective-permute-start.2) | collective-permute-done | bytes 80032 | tf_op jit(solution)/shard_map/ppermute | solution.py:336
  12.9 0.8 collective-permute-done.3.refs_3_
  13.7 1.6 %lay.1.refs_0_ = bf16[200,896]{1,0:T(8,128)(2,1)S(1)} custom-call(s32[3]{0:T(128)S(1)} %pad_add_fusion.at, bf16[2,200,100]{2,1,0:T(8,128)(2,1)S(1)} %pad_maximum_fusion.refs_0_, bf16[2,200,100]{2,1,0:T(8,128)(2,1)S(1)} %collective-permute-done.1.refs_1_, bf16[2,200,100]{2,1,0:T(8,128)(2,1)S(1)} %collective-permute-done.2.refs_2_, ...), custom_call_target="tpu_custom_call" | custom-call | tf_op jit(solution)/shard_map/lay/pallas_call | solution.py:57
  15.3 1.0 collective-permute-start.4
  16.2 4.0 %collective-permute-start.10 = (bf16[200,896]{1,0:T(8,128)(2,1)S(1)}, bf16[200,896]{1,0:T(8,128)(2,1)}, u32[]{:S(2)}, u32[]{:S(2)}) collective-permute-start(bf16[200,896]{1,0:T(8,128)(2,1)S(1)} %lay.1.refs_0_), channel_id=1, source_target_pairs={{0,56},{8,0},{16,8},{24,16},{32,24},{40,32},{48,40},{56,48},{1,57}... | collective-permute-start | bytes 1075208 | tf_op jit(solution)/shard_map/ppermute | solution.py:343
  20.3 7.5 %collective-permute-done.4.refs_0_ = bf16[200,896]{1,0:T(8,128)(2,1)S(1)} collective-permute-done((bf16[200,896]{1,0:T(8,128)(2,1)S(1)}, bf16[200,896]{1,0:T(8,128)(2,1)S(1)}, u32[]{:S(2)}, u32[]{:S(2)}) %collective-permute-start.4) | collective-permute-done | bytes 358432 | tf_op jit(solution)/shard_map/ppermute | solution.py:343
  27.7 2.7 %collective-permute-start.11 = (bf16[200,896]{1,0:T(8,128)(2,1)}, bf16[200,896]{1,0:T(8,128)(2,1)}, u32[]{:S(2)}, u32[]{:S(2)}) collective-permute-start(bf16[200,896]{1,0:T(8,128)(2,1)} %collective-permute-done.10.refs_2_), channel_id=1, source_target_pairs={{0,56},{8,0},{16,8},{24,16},{32,24},{40,32},{48,40},{56,48},{1,57}... | collective-permute-start | bytes 1075208 | tf_op jit(solution)/shard_map/ppermute | solution.py:343
  30.4 6.8 %collective-permute-done.5.refs_0_ = bf16[200,896]{1,0:T(8,128)(2,1)} collective-permute-done((bf16[200,896]{1,0:T(8,128)(2,1)S(1)}, bf16[200,896]{1,0:T(8,128)(2,1)}, u32[]{:S(2)}, u32[]{:S(2)}) %collective-permute-start.5) | collective-permute-done | bytes 358432 | tf_op jit(solution)/shard_map/ppermute | solution.py:343
  37.2 2.6 %collective-permute-start.18 = (bf16[200,896]{1,0:T(8,128)(2,1)S(1)}, bf16[200,896]{1,0:T(8,128)(2,1)}, u32[]{:S(2)}, u32[]{:S(2)}) collective-permute-start(bf16[200,896]{1,0:T(8,128)(2,1)S(1)} %lay.1.refs_0_), channel_id=1, source_target_pairs={{0,1},{1,0},{2,3},{3,2},{4,5},{5,4},{6,7},{7,6},{8,9},{9,8},{10,11... | collective-permute-start | bytes 1075208 | tf_op jit(solution)/shard_map/ppermute | solution.py:348
  39.8 0.7 copy-done.4
  40.6 0.7 copy-done.6
  41.8 3.0 %collective-permute-start.12 = (bf16[200,896]{1,0:T(8,128)(2,1)}, bf16[200,896]{1,0:T(8,128)(2,1)}, u32[]{:S(2)}, u32[]{:S(2)}) collective-permute-start(bf16[200,896]{1,0:T(8,128)(2,1)} %collective-permute-done.11.refs_2_), channel_id=1, source_target_pairs={{0,56},{8,0},{16,8},{24,16},{32,24},{40,32},{48,40},{56,48},{1,57}... | collective-permute-start | bytes 1075208 | tf_op jit(solution)/shard_map/ppermute | solution.py:343
  44.8 1.2 %collective-permute-done.6.refs_0_ = bf16[200,896]{1,0:T(8,128)(2,1)} collective-permute-done((bf16[200,896]{1,0:T(8,128)(2,1)}, bf16[200,896]{1,0:T(8,128)(2,1)}, u32[]{:S(2)}, u32[]{:S(2)}) %collective-permute-start.6) | collective-permute-done | bytes 358432 | tf_op jit(solution)/shard_map/ppermute | solution.py:343
  46.0 1.3 %select_reduce_fusion = (f32[400]{0:T(512)}, f32[400]{0:T(512)}) fusion(s32[400]{0:T(512)S(1)} %get-tuple-element.136, f32[40]{0:T(128)} %param.15, s32[400]{0:T(512)S(1)} %get-tuple-element.137), kind=kLoop, calls=%fused_computation.9 | loop fusion | flops 95200 | bytes 6560 | tf_op jit(solution)/shard_map/reduce_sum | solution.py:355
  48.1 0.8 dynamic_slice.11
  49.5 0.7 add.76
  50.2 3.5 %collective-permute-start.14 = (bf16[200,896]{1,0:T(8,128)(2,1)}, bf16[200,896]{1,0:T(8,128)(2,1)}, u32[]{:S(2)}, u32[]{:S(2)}) collective-permute-start(bf16[200,896]{1,0:T(8,128)(2,1)} %collective-permute-done.5.refs_0_), channel_id=1, source_target_pairs={{0,1},{1,0},{2,3},{3,2},{4,5},{5,4},{6,7},{7,6},{8,9},{9,8},{10,11... | collective-permute-start | bytes 1075208 | tf_op jit(solution)/shard_map/ppermute | solution.py:348
  53.7 0.7 copy-done.8
  54.8 3.1 %gram.1 = (f32[1600,300]{1,0:T(8,128)S(1)}, f32[1,128]{1,0:T(1,128)S(1)}, bf16[1,300,4,896]{3,2,1,0:T(4,128)(2,1)S(1)}) custom-call(s32[3]{0:T(128)S(1)} %pad_add_fusion.at, f32[1,300]{1,0:T(1,128)S(1)} %broadcast_in_dim.26.virt, f32[1600,1]{1,0:T(8,128)S(1)} %sub.86.row_term, bf16[2,400,4,300]{3,2,1,0:T(4,128)(2,1)S(1)} %copy-done, ...), custom_call_target="tpu_custom_call" | custom-call | flops 9600000 | bytes 8000000 | tf_op jit(solution)/shard_map/gram/pallas_call | solution.py:184
  58.6 3.4 %multiply.4 = (f32[400,1200]{1,0:T(8,128)S(1)}, bf16[2,300,4,896]{3,2,1,0:T(4,128)(2,1)S(1)}) custom-call(s32[3]{0:T(128)S(1)} %pad_add_fusion.at, bf16[200,896]{1,0:T(8,128)(2,1)S(1)} %copy-done.5, bf16[200,896]{1,0:T(8,128)(2,1)} %collective-permute-done.18.refs_1_, bf16[300,4,6400]{2,1,0:T(4,128)(2,1)} %bitcast.24, ...), custom_call_target="tpu_custom_call" | custom-call | flops 860160000 | bytes 3000000 | tf_op jit(solution)/shard_map/multiply/pallas_call | solution.py:120
  62.5 3.8 %multiply.5 = (f32[400,1200]{1,0:T(8,128)S(1)}, bf16[2,300,4,896]{3,2,1,0:T(4,128)(2,1)S(1)}) custom-call(s32[3]{0:T(128)S(1)} %pad_add_fusion.at, bf16[200,896]{1,0:T(8,128)(2,1)S(1)} %copy-done.7, bf16[200,896]{1,0:T(8,128)(2,1)S(1)} %copy-done.9, bf16[200,896]{1,0:T(8,128)(2,1)} %collective-permute-done.10.refs_2_, ...), custom_call_target="tpu_custom_call", output_to_operand_aliasing={{0}: (7, {})} | custom-call | flops 1720320000 | bytes 6000000 | tf_op jit(solution)/shard_map/multiply/pallas_call | solution.py:120
  66.4 4.1 %multiply.6 = (f32[400,1200]{1,0:T(8,128)S(1)}, bf16[2,300,4,896]{3,2,1,0:T(4,128)(2,1)S(1)}) custom-call(s32[3]{0:T(128)S(1)} %pad_add_fusion.at, bf16[200,896]{1,0:T(8,128)(2,1)} %collective-permute-done.5.refs_0_, bf16[200,896]{1,0:T(8,128)(2,1)} %collective-permute-done.14.refs_1_, ...), custom_call_target="tpu_custom_call", output_to_operand_aliasing={{0}: (7, {})} | custom-call | flops 1720320000 | bytes 6000000 | tf_op jit(solution)/shard_map/multiply/pallas_call | solution.py:120
  70.5 5.2 %multiply.7 = (f32[400,1200]{1,0:T(8,128)S(1)}, bf16[1,300,4,896]{3,2,1,0:T(4,128)(2,1)S(1)}) custom-call(s32[3]{0:T(128)S(1)} %pad_add_fusion.at, bf16[200,896]{1,0:T(8,128)(2,1)} %collective-permute-done.6.refs_0_, bf16[200,896]{1,0:T(8,128)(2,1)S(1)} %collective-permute-done.9.refs_1_, ...), custom_call_target="tpu_custom_call", output_to_operand_aliasing={{0}: (7, {})} | custom-call | flops 1720320000 | bytes 6000000 | tf_op jit(solution)/shard_map/multiply/pallas_call | solution.py:120
  75.7 8.6 %last.1 = (bf16[400,4,300]{2,1,0:T(4,128)(2,1)S(1)}, f32[256,1,128]{2,1,0:T(1,128)S(1)}) custom-call(s32[3]{0:T(128)S(1)} %pad_add_fusion.at, bf16[200,896]{1,0:T(8,128)(2,1)} %collective-permute-done.7.refs_0_, bf16[200,896]{1,0:T(8,128)(2,1)S(1)} %collective-permute-done.8.refs_1_, bf16[1,300,4,896]{3,2,1,0:T(4,128)(2,1)S(1)} %get-tuple-element.71.refs_2_, ...), custom_call_target="tpu_custom_call" | custom-call | tf_op jit(solution)/shard_map/last/pallas_call | solution.py:256
  84.3 22.7 %all_to_all.5.gathered = f32[256,1,128]{2,1,0:T(1,128)S(1)} all-to-all(f32[256,1,128]{2,1,0:T(1,128)S(1)} %get-tuple-element.76), channel_id=1, replica_groups=mesh['x'=4,'z'=8,'y'=4,'c'=2] {'x','z','y','c'}, dimensions={0} | all-to-all | bytes 262144 | tf_op jit(solution)/shard_map/all_to_all | solution.py:371
  107.0 3.4 %finish.1 = (bf16[400,4,300]{2,1,0:T(4,128)(2,1)}, f32[2]{0:T(128)S(1)}, f32[1]{0:T(128)}) custom-call(f32[256,1,128]{2,1,0:T(1,128)S(1)} %all_to_all.5.gathered, f32[1]{0:T(128)} %copy.28.refs_4_.shift, f32[1600,300]{1,0:T(8,128)S(1)} %get-tuple-element.73.refs_5_.inverse, bf16[400,4,300]{2,1,0:T(4,128)(2,1)S(1)} %get-tuple-element.151.sigma, ...), custom_call_target="tpu_custom_call" | custom-call | tf_op jit(solution)/shard_map/finish/pallas_call | solution.py:309
  (50 shorter events, 4.1 us)
Async XLA Ops:
  0.6 54.1 %copy-start = (bf16[2,400,4,300]{3,2,1,0:T(4,128)(2,1)S(1)}, bf16[2,400,4,300]{3,2,1,0:T(4,128)(2,1)}, u32[]{:S(2)}) copy-start(bf16[2,400,4,300]{3,2,1,0:T(4,128)(2,1)} %images.3) | copy-start | bytes 5760004
  1.6 4.2 %collective-permute-start = (bf16[200,100]{1,0:T(8,128)(2,1)S(1)}, bf16[200,100]{1,0:T(8,128)(2,1)S(1)}, u32[]{:S(2)}, u32[]{:S(2)}) collective-permute-start(bf16[200,100]{1,0:T(8,128)(2,1)S(1)} %get-tuple-element.135), channel_id=1, source_target_pairs={{0,1},{1,0},{2,3},{3,2},{4,5},{5,4},{6,7},{7,6},{8,9},{9,8},{10,11... | collective-permute-start | bytes 120008 | tf_op jit(solution)/shard_map/ppermute | solution.py:335
  5.8 5.8 %collective-permute-start.1 = (bf16[2,200,100]{2,1,0:T(8,128)(2,1)S(1)}, bf16[2,200,100]{2,1,0:T(8,128)(2,1)S(1)}, u32[]{:S(2)}, u32[]{:S(2)}) collective-permute-start(bf16[2,200,100]{2,1,0:T(8,128)(2,1)S(1)} %pad_maximum_fusion.refs_0_), channel_id=1, source_target_pairs={{0,2},{2,4},{4,6},{6,0},{1,3},{3,5},{5,7},{7,1},{8,10},{10,12},{12... | collective-permute-start | bytes 240008 | tf_op jit(solution)/shard_map/ppermute | solution.py:336
  5.9 7.0 %collective-permute-start.2 = (bf16[2,200,100]{2,1,0:T(8,128)(2,1)S(1)}, bf16[2,200,100]{2,1,0:T(8,128)(2,1)S(1)}, u32[]{:S(2)}, u32[]{:S(2)}) collective-permute-start(bf16[2,200,100]{2,1,0:T(8,128)(2,1)S(1)} %pad_maximum_fusion.refs_0_), channel_id=1, source_target_pairs={{0,4},{2,6},{4,0},{6,2},{1,5},{3,7},{5,1},{7,3},{8,12},{10,14},{12... | collective-permute-start | bytes 240008 | tf_op jit(solution)/shard_map/ppermute | solution.py:336
  8.1 5.6 %collective-permute-start.3 = (bf16[2,200,100]{2,1,0:T(8,128)(2,1)S(1)}, bf16[2,200,100]{2,1,0:T(8,128)(2,1)S(1)}, u32[]{:S(2)}, u32[]{:S(2)}) collective-permute-start(bf16[2,200,100]{2,1,0:T(8,128)(2,1)S(1)} %pad_maximum_fusion.refs_0_), channel_id=1, source_target_pairs={{0,6},{2,0},{4,2},{6,4},{1,7},{3,1},{5,3},{7,5},{8,14},{10,8},{12,... | collective-permute-start | bytes 240008 | tf_op jit(solution)/shard_map/ppermute | solution.py:336
  15.3 12.4 %collective-permute-start.4 = (bf16[200,896]{1,0:T(8,128)(2,1)S(1)}, bf16[200,896]{1,0:T(8,128)(2,1)S(1)}, u32[]{:S(2)}, u32[]{:S(2)}) collective-permute-start(bf16[200,896]{1,0:T(8,128)(2,1)S(1)} %lay.1.refs_0_), channel_id=1, source_target_pairs={{0,8},{8,16},{16,24},{24,32},{32,40},{40,48},{48,56},{56,0},{1,9},... | collective-permute-start | bytes 1075208 | tf_op jit(solution)/shard_map/ppermute | solution.py:343
  16.2 11.5 %collective-permute-start.10 = (bf16[200,896]{1,0:T(8,128)(2,1)S(1)}, bf16[200,896]{1,0:T(8,128)(2,1)}, u32[]{:S(2)}, u32[]{:S(2)}) collective-permute-start(bf16[200,896]{1,0:T(8,128)(2,1)S(1)} %lay.1.refs_0_), channel_id=1, source_target_pairs={{0,56},{8,0},{16,8},{24,16},{32,24},{40,32},{48,40},{56,48},{1,57}... | collective-permute-start | bytes 1075208 | tf_op jit(solution)/shard_map/ppermute | solution.py:343
  27.7 9.5 %collective-permute-start.5 = (bf16[200,896]{1,0:T(8,128)(2,1)S(1)}, bf16[200,896]{1,0:T(8,128)(2,1)}, u32[]{:S(2)}, u32[]{:S(2)}) collective-permute-start(bf16[200,896]{1,0:T(8,128)(2,1)S(1)} %collective-permute-done.4.refs_0_), channel_id=1, source_target_pairs={{0,8},{8,16},{16,24},{24,32},{32,40},{40,48},{48,56},{56,0},{1,9},... | collective-permute-start | bytes 1075208 | tf_op jit(solution)/shard_map/ppermute | solution.py:343
  27.7 14.1 %collective-permute-start.11 = (bf16[200,896]{1,0:T(8,128)(2,1)}, bf16[200,896]{1,0:T(8,128)(2,1)}, u32[]{:S(2)}, u32[]{:S(2)}) collective-permute-start(bf16[200,896]{1,0:T(8,128)(2,1)} %collective-permute-done.10.refs_2_), channel_id=1, source_target_pairs={{0,56},{8,0},{16,8},{24,16},{32,24},{40,32},{48,40},{56,48},{1,57}... | collective-permute-start | bytes 1075208 | tf_op jit(solution)/shard_map/ppermute | solution.py:343
  37.2 8.8 %collective-permute-start.6 = (bf16[200,896]{1,0:T(8,128)(2,1)}, bf16[200,896]{1,0:T(8,128)(2,1)}, u32[]{:S(2)}, u32[]{:S(2)}) collective-permute-start(bf16[200,896]{1,0:T(8,128)(2,1)} %collective-permute-done.5.refs_0_), channel_id=1, source_target_pairs={{0,8},{8,16},{16,24},{24,32},{32,40},{40,48},{48,56},{56,0},{1,9},... | collective-permute-start | bytes 1075208 | tf_op jit(solution)/shard_map/ppermute | solution.py:343
  37.2 13.0 %collective-permute-start.18 = (bf16[200,896]{1,0:T(8,128)(2,1)S(1)}, bf16[200,896]{1,0:T(8,128)(2,1)}, u32[]{:S(2)}, u32[]{:S(2)}) collective-permute-start(bf16[200,896]{1,0:T(8,128)(2,1)S(1)} %lay.1.refs_0_), channel_id=1, source_target_pairs={{0,1},{1,0},{2,3},{3,2},{4,5},{5,4},{6,7},{7,6},{8,9},{9,8},{10,11... | collective-permute-start | bytes 1075208 | tf_op jit(solution)/shard_map/ppermute | solution.py:348
  39.8 0.7 copy-start.4
  40.6 13.1 %collective-permute-start.16 = (bf16[200,896]{1,0:T(8,128)(2,1)S(1)}, bf16[200,896]{1,0:T(8,128)(2,1)S(1)}, u32[]{:S(2)}, u32[]{:S(2)}) collective-permute-start(bf16[200,896]{1,0:T(8,128)(2,1)S(1)} %collective-permute-done.4.refs_0_), channel_id=1, source_target_pairs={{0,1},{1,0},{2,3},{3,2},{4,5},{5,4},{6,7},{7,6},{8,9},{9,8},{10,11... | collective-permute-start | bytes 1075208 | tf_op jit(solution)/shard_map/ppermute | solution.py:348
  40.6 0.7 copy-start.6
  41.3 16.6 %collective-permute-start.17 = (bf16[200,896]{1,0:T(8,128)(2,1)}, bf16[200,896]{1,0:T(8,128)(2,1)}, u32[]{:S(2)}, u32[]{:S(2)}) collective-permute-start(bf16[200,896]{1,0:T(8,128)(2,1)} %collective-permute-done.10.refs_2_), channel_id=1, source_target_pairs={{0,1},{1,0},{2,3},{3,2},{4,5},{5,4},{6,7},{7,6},{8,9},{9,8},{10,11... | collective-permute-start | bytes 1075208 | tf_op jit(solution)/shard_map/ppermute | solution.py:348
  41.8 16.6 %collective-permute-start.12 = (bf16[200,896]{1,0:T(8,128)(2,1)}, bf16[200,896]{1,0:T(8,128)(2,1)}, u32[]{:S(2)}, u32[]{:S(2)}) collective-permute-start(bf16[200,896]{1,0:T(8,128)(2,1)} %collective-permute-done.11.refs_2_), channel_id=1, source_target_pairs={{0,56},{8,0},{16,8},{24,16},{32,24},{40,32},{48,40},{56,48},{1,57}... | collective-permute-start | bytes 1075208 | tf_op jit(solution)/shard_map/ppermute | solution.py:343
  46.0 16.0 %collective-permute-start.7 = (bf16[200,896]{1,0:T(8,128)(2,1)}, bf16[200,896]{1,0:T(8,128)(2,1)}, u32[]{:S(2)}, u32[]{:S(2)}) collective-permute-start(bf16[200,896]{1,0:T(8,128)(2,1)} %collective-permute-done.6.refs_0_), channel_id=1, source_target_pairs={{0,8},{8,16},{16,24},{24,32},{32,40},{40,48},{48,56},{56,0},{1,9},... | collective-permute-start | bytes 1075208 | tf_op jit(solution)/shard_map/ppermute | solution.py:343
  50.2 16.2 %collective-permute-start.14 = (bf16[200,896]{1,0:T(8,128)(2,1)}, bf16[200,896]{1,0:T(8,128)(2,1)}, u32[]{:S(2)}, u32[]{:S(2)}) collective-permute-start(bf16[200,896]{1,0:T(8,128)(2,1)} %collective-permute-done.5.refs_0_), channel_id=1, source_target_pairs={{0,1},{1,0},{2,3},{3,2},{4,5},{5,4},{6,7},{7,6},{8,9},{9,8},{10,11... | collective-permute-start | bytes 1075208 | tf_op jit(solution)/shard_map/ppermute | solution.py:348
  53.6 0.7 copy-start.8
  54.4 12.0 %collective-permute-start.15 = (bf16[200,896]{1,0:T(8,128)(2,1)}, bf16[200,896]{1,0:T(8,128)(2,1)}, u32[]{:S(2)}, u32[]{:S(2)}) collective-permute-start(bf16[200,896]{1,0:T(8,128)(2,1)} %collective-permute-done.11.refs_2_), channel_id=1, source_target_pairs={{0,1},{1,0},{2,3},{3,2},{4,5},{5,4},{6,7},{7,6},{8,9},{9,8},{10,11... | collective-permute-start | bytes 1075208 | tf_op jit(solution)/shard_map/ppermute | solution.py:348
  54.7 3.8 %copy-start.5 = (bf16[200,896]{1,0:T(8,128)(2,1)S(1)}, bf16[200,896]{1,0:T(8,128)(2,1)}, u32[]{:S(2)}) copy-start(bf16[200,896]{1,0:T(8,128)(2,1)} %copy-done.4) | copy-start | bytes 1075204
  57.9 12.6 %collective-permute-start.9 = (bf16[200,896]{1,0:T(8,128)(2,1)}, bf16[200,896]{1,0:T(8,128)(2,1)S(1)}, u32[]{:S(2)}, u32[]{:S(2)}) collective-permute-start(bf16[200,896]{1,0:T(8,128)(2,1)} %collective-permute-done.6.refs_0_), channel_id=1, source_target_pairs={{0,1},{1,0},{2,3},{3,2},{4,5},{5,4},{6,7},{7,6},{8,9},{9,8},{10,11... | collective-permute-start | bytes 1075208 | tf_op jit(solution)/shard_map/ppermute | solution.py:348
  58.5 12.0 %collective-permute-start.13 = (bf16[200,896]{1,0:T(8,128)(2,1)}, bf16[200,896]{1,0:T(8,128)(2,1)S(1)}, u32[]{:S(2)}, u32[]{:S(2)}) collective-permute-start(bf16[200,896]{1,0:T(8,128)(2,1)} %collective-permute-done.12.refs_2_), channel_id=1, source_target_pairs={{0,1},{1,0},{2,3},{3,2},{4,5},{5,4},{6,7},{7,6},{8,9},{9,8},{10,11... | collective-permute-start | bytes 1075208 | tf_op jit(solution)/shard_map/ppermute | solution.py:348
  58.6 3.9 %copy-start.7 = (bf16[200,896]{1,0:T(8,128)(2,1)S(1)}, bf16[200,896]{1,0:T(8,128)(2,1)}, u32[]{:S(2)}) copy-start(bf16[200,896]{1,0:T(8,128)(2,1)} %copy-done.6) | copy-start | bytes 1075204
  58.6 3.9 %copy-start.9 = (bf16[200,896]{1,0:T(8,128)(2,1)S(1)}, bf16[200,896]{1,0:T(8,128)(2,1)}, u32[]{:S(2)}) copy-start(bf16[200,896]{1,0:T(8,128)(2,1)} %copy-done.8) | copy-start | bytes 1075204
  62.0 13.7 %collective-permute-start.8 = (bf16[200,896]{1,0:T(8,128)(2,1)}, bf16[200,896]{1,0:T(8,128)(2,1)S(1)}, u32[]{:S(2)}, u32[]{:S(2)}) collective-permute-start(bf16[200,896]{1,0:T(8,128)(2,1)} %collective-permute-done.7.refs_0_), channel_id=1, source_target_pairs={{0,1},{1,0},{2,3},{3,2},{4,5},{5,4},{6,7},{7,6},{8,9},{9,8},{10,11... | collective-permute-start | bytes 1075208 | tf_op jit(solution)/shard_map/ppermute | solution.py:348
  70.5 5.2 %copy-start.1 = (bf16[400,4,300]{2,1,0:T(4,128)(2,1)S(1)}, bf16[400,4,300]{2,1,0:T(4,128)(2,1)}, u32[]{:S(2)}) copy-start(bf16[400,4,300]{2,1,0:T(4,128)(2,1)} %current.1) | copy-start | bytes 2880004
  70.5 5.2 %copy-start.3 = (bf16[2,400,4,300]{3,2,1,0:T(4,128)(2,1)S(1)}, bf16[2,400,4,300]{3,2,1,0:T(4,128)(2,1)}, u32[]{:S(2)}) copy-start(bf16[2,400,4,300]{3,2,1,0:T(4,128)(2,1)} %refs_7_.1) | copy-start | bytes 5760004
  84.3 26.1 %copy-start.2 = (bf16[400,4,300]{2,1,0:T(4,128)(2,1)}, bf16[400,4,300]{2,1,0:T(4,128)(2,1)S(1)}, u32[]{:S(2)}) copy-start(bf16[400,4,300]{2,1,0:T(4,128)(2,1)S(1)} %get-tuple-element.151.sigma) | copy-start | bytes 2880004
  107.0 3.4 %copy-start.10 = (f32[300]{0:T(512)S(1)}, f32[300]{0:T(512)}, u32[]{:S(2)}) copy-start(f32[300]{0:T(512)} %param.16) | copy-start | bytes 3604
  111.0 0.5 copy-start.11
